TPU v7x, 256 devices: a whole 4x4x8 slice. The times are simulated.
256 devices in a mesh: row: 8 (over z), col: 32 (over y, x, core).
Axes of the slice: x: 4, y: 4, z: 8, core: 2. Of those that a mesh axis runs over, the one named last changes fastest.
Arguments:
- ancestor_inverse: bfloat16 [24576, 24576], P('row', 'col'), may hold values from -6 to 6
- factor_slots: bfloat16 [3, 16384, 512], P(None, ('row', 'col')), may hold values from -0.25 to 0.25
- slot_tiles: int32 [3, 64], replicated, may hold values from -1 to 95, as said below
- parent_factor: bfloat16 [2, 512, 512], replicated, may hold values from -0.25 to 0.25
- diag_inverse: float32 [3, 512, 512], replicated, may hold values from -6 to 6
Outputs:
- inverse_panels: bfloat16 [3, 24576, 512], P(None, ('row', 'col'))
- diag_blocks: float32 [3, 512, 512], replicated
- parent_blocks: float32 [2, 512, 512], replicated
Inputs may be any that keep to these rules, and one draw needn't show every extreme that they name: `slot_tiles`: entries b * 2 to b * 2 + 1 of a supernode's row are the slots of column block b: each is -1 (empty) or names a tile from b * 3 to b * 3 + 2, no tile twice; in each supernode some block has all its slots filled. `factor_slots`: rows of an empty slot are not part of the factor.
All inputs are finite; a program needn't handle non-finite values.
Results may differ from a plain program's by a relative error of at most 0.00075.
Values may be sent and summed in bfloat16 or wider, within the bound.
No kernel may reach another device: no remote copies, remote signals or barrier semaphores. Data moves between devices by JAX's collectives and lax.ppermute only.
A program may use at most 128 MiB of HBM per device.

v0:
```python
import jax
import jax.numpy as jnp
from jax import lax
from jax.sharding import PartitionSpec as P

TILE = 256
CAP = 2
exact_mode = lax.Precision.HIGHEST


def spread(shard, axis, root):
    mine = lax.axis_index(axis) == root
    return lax.psum(jnp.where(mine, shard, jnp.zeros_like(shard)), axis)


def padded_block(slot_data, slot_ids, block_index, tiles_per_block, tile_rows):
    local_tile = slot_ids - block_index * tiles_per_block
    pieces = []
    for tile_index in range(tiles_per_block):
        chosen = jnp.zeros((tile_rows, slot_data.shape[1]), slot_data.dtype)
        for member in range(slot_ids.shape[0]):
            chosen = jnp.where(
                local_tile[member] == tile_index,
                slot_data[member * tile_rows : (member + 1) * tile_rows],
                chosen,
            )
        pieces.append(chosen)
    return jnp.concatenate(pieces, axis=0)


def chosen_columns(inverse_block, slot_ids, block_index, tiles_per_block, tile_rows):
    local_tile = jnp.clip(slot_ids - block_index * tiles_per_block, 0, tiles_per_block - 1)
    pieces = [
        lax.dynamic_slice_in_dim(inverse_block, local_tile[member] * tile_rows, tile_rows, 1)
        for member in range(slot_ids.shape[0])
    ]
    return jnp.concatenate(pieces, axis=1)


def masked_rows(slot_data, slot_ids, tile_rows):
    live_rows = jnp.repeat(slot_ids >= 0, tile_rows)
    return jnp.where(live_rows[:, None], slot_data, jnp.zeros_like(slot_data))


def on_device(ancestor_inverse, factor_slots, slot_tiles, parent_factor, diag_inverse):
    row_count = lax.axis_size("row")
    col_count = lax.axis_size("col")
    row_index = lax.axis_index("row")
    col_index = lax.axis_index("col")
    block_rows, block_cols = ancestor_inverse.shape
    tile_rows = TILE
    tiles_per_block = block_cols // tile_rows
    node_count = factor_slots.shape[0]
    slot_count = CAP
    slot_rows = slot_count * tile_rows
    groups_per_row = col_count // row_count
    panel_rows = block_rows // col_count
    own_block = row_index * groups_per_row + col_index // row_count
    own_offset = col_index % row_count * panel_rows
    slot_start = col_index % groups_per_row * slot_rows
    owner_row = col_index // groups_per_row

    def finish(node, first_total, second_total, prev_diag):
        if node == 0:
            return (diag_inverse[0] - first_total, None)
        parent_link = parent_factor[node - 1].astype(jnp.float32)
        upper = -(second_total + jnp.dot(prev_diag, parent_link, precision=exact_mode))
        diagonal = (
            diag_inverse[node] - first_total - jnp.dot(parent_link.T, upper, precision=exact_mode)
        )
        return (diagonal, upper)

    def node_sums(node, first_part, second_part):
        if node == 0:
            return (lax.psum(first_part, ("row", "col")), None)
        return lax.psum((first_part, second_part), ("row", "col"))

    panels = []
    diagonals = []
    parents = []
    previous = None
    prev_diag = None
    for node in range(node_count):
        row_slots = lax.all_gather(factor_slots[node], "col", axis=0, tiled=True)
        mine = lax.dynamic_slice_in_dim(row_slots, slot_start, slot_rows, 0)
        col_slots = spread(mine, "row", owner_row)
        tiles_node = slot_tiles[node]
        col_ids = lax.dynamic_slice_in_dim(tiles_node, col_index * slot_count, slot_count)
        prepare_columns = chosen_columns(
            ancestor_inverse, col_ids, col_index, tiles_per_block, tile_rows
        )
        prepare_weights = masked_rows(col_slots, col_ids, tile_rows)
        own_ids = lax.dynamic_slice_in_dim(tiles_node, own_block * slot_count, slot_count)
        own_slots = lax.dynamic_slice_in_dim(
            row_slots, col_index // row_count * slot_rows, slot_rows, 0
        )
        own_padded = padded_block(own_slots, own_ids, own_block, tiles_per_block, tile_rows)
        own_rows = lax.dynamic_slice_in_dim(own_padded, own_offset, panel_rows, 0)
        row_padded = None
        columns, weights, own_rows, row_padded = (
            prepare_columns,
            prepare_weights,
            own_rows.astype(jnp.float32),
            row_padded,
        )
        second_part = None
        if node > 0:
            second_part = jnp.dot(previous.T, own_rows, precision=exact_mode)
        summed = lax.psum_scatter(
            jnp.dot(columns, weights, preferred_element_type=jnp.float32),
            "col",
            scatter_dimension=0,
            tiled=True,
        )
        column = -summed
        if node > 0:
            advance_parent_link = parent_factor[node - 1].astype(jnp.float32)
            column = column - jnp.dot(previous, advance_parent_link, precision=exact_mode)
        first_part = jnp.dot(own_rows.T, column, precision=exact_mode)
        first_total, second_total = node_sums(node, first_part, second_part)
        diagonal, upper = finish(node, first_total, second_total, prev_diag)
        panels.append(column.astype(jnp.bfloat16))
        diagonals.append(diagonal)
        if node > 0:
            parents.append(upper)
        previous = column
        prev_diag = diagonal
    return (jnp.stack(panels), jnp.stack(diagonals), jnp.stack(parents))


def solution(mesh):
    placed = (P("row", "col"), P(None, ("row", "col"), None), P(), P(), P())
    return jax.shard_map(
        on_device,
        mesh=mesh,
        in_specs=placed,
        out_specs=(P(None, ("row", "col"), None), P(), P()),
        check_vma=False,
    )
```

profile of v0, /device:TPU:8, one launch (start us, length us, event | category | flops | bytes accessed | tf_op | source)
XLA Modules:
  0.0 841.9 jit_solution(13287973406344088835)
XLA Ops:
  7.2 1.6 fusion.71
  10.4 51.9 %all-gather.9.cloned.1.call-done = bf16[1,2048,512]{2,1,0:T(8,128)(2,1)} async-done(((bf16[1,64,512]{2,1,0:T(8,128)(2,1)}), bf16[1,2048,512]{2,1,0:T(8,128)(2,1)}) %all-gather.9.cloned.1.call-update) | async-done | bytes 2097168 | tf_op jit(solution)/shard_map/all_gather | solution.py:84
  62.3 1.9 select_bitcast_fusion.1
  64.2 49.2 %all-gather.7.cloned.1.call-done = bf16[1,2048,512]{2,1,0:T(8,128)(2,1)} async-done(((bf16[1,64,512]{2,1,0:T(8,128)(2,1)}), bf16[1,2048,512]{2,1,0:T(8,128)(2,1)}) %all-gather.7.cloned.1.call-update) | async-done | bytes 2097168 | tf_op jit(solution)/shard_map/all_gather | solution.py:84
  113.4 1.9 select_bitcast_fusion.2
  115.3 49.2 %all-gather.11.cloned.1.call-done = bf16[1,2048,512]{2,1,0:T(8,128)(2,1)} async-done(((bf16[1,64,512]{2,1,0:T(8,128)(2,1)}), bf16[1,2048,512]{2,1,0:T(8,128)(2,1)}) %all-gather.11.cloned.1.call-update) | async-done | bytes 2097168 | tf_op jit(solution)/shard_map/all_gather | solution.py:84
  164.5 1.9 select_bitcast_fusion
  172.6 6.8 constant_dynamic-slice_fusion.4
  179.5 66.0 %all-reduce.7.cloned.1.call-done = (bf16[512,512]{1,0:T(8,128)(2,1)}, bf16[512,512]{1,0:T(8,128)(2,1)}, bf16[512,512]{1,0:T(8,128)(2,1)}) async-done(((bf16[512,512]{1,0:T(8,128)(2,1)}, bf16[512,512]{1,0:T(8,128)(2,1)}, bf16[512,512]{1,0:T(8,128)(2,1)}), (bf16[512,512]{1,0:T(8,128)(2,1)}, bf16[512,512]{1,0:T(8,128)(2,1)}, bf16[512,512]{1,0:T(8,128)(2,1)})) %all-reduce.7.cloned.1.call-update) | async-done | bytes 1572880 | tf_op jit(solution)/shard_map/psum | solution.py:13
  245.4 6.5 fusion.4
  252.2 6.5 fusion
  258.8 5.5 fusion.8
  277.3 1.2 select_bitcast_fusion.8
  278.5 2.0 select_bitcast_fusion.10
  280.5 1.2 select_bitcast_fusion.5
  281.7 63.3 %reduce-scatter.6.cloned.1.call-done = f32[96,512]{1,0:T(8,128)} async-done(((f32[3072,512]{1,0:T(8,128)}), f32[96,512]{1,0:T(8,128)}) %reduce-scatter.6.cloned.1.call-update) | async-done | bytes 196624 | tf_op jit(solution)/shard_map/reduce_scatter | solution.py:109
  345.0 97.1 %reduce-scatter.4.cloned.1.call-done = f32[96,512]{1,0:T(8,128)} async-done(((f32[3072,512]{1,0:T(8,128)}), f32[96,512]{1,0:T(8,128)}) %reduce-scatter.4.cloned.1.call-update) | async-done | bytes 196624 | tf_op jit(solution)/shard_map/reduce_scatter | solution.py:109
  442.1 1.4 convolution_subtract_fusion.1
  443.5 1.7 fusion.69
  445.2 94.2 %reduce-scatter.8.cloned.1.call-done = f32[96,512]{1,0:T(8,128)} async-done(((f32[3072,512]{1,0:T(8,128)}), f32[96,512]{1,0:T(8,128)}) %reduce-scatter.8.cloned.1.call-update) | async-done | bytes 196624 | tf_op jit(solution)/shard_map/reduce_scatter | solution.py:109
  539.4 1.3 convolution_subtract_fusion
  540.7 1.7 fusion.67
  542.5 1.7 fusion.64
  544.2 1.7 fusion.39
  545.8 1.8 fusion.41
  548.5 274.5 %all-reduce.5.cloned.1.call-done = (f32[512,512]{1,0:T(8,128)}, f32[512,512]{1,0:T(8,128)}, f32[512,512]{1,0:T(8,128)}, f32[512,512]{1,0:T(8,128)}, f32[512,512]{1,0:T(8,128)}) async-done(((f32[512,512]{1,0:T(8,128)}, f32[512,512]{1,0:T(8,128)}, f32[512,512]{1,0:T(8,128)}, f32[512,512]{1,0:T(8,128)}, f32[512,512]{1,0:T(8,128)}), (f32[512,512]{1,0:T(8,128)}, f32[512,512]{1,0:T(8,128)}, f32[512,512]{1,0:T(8,128)}, ...) | async-done | bytes 5242896 | tf_op jit(solution)/shard_map/psum | solution.py:76
  823.1 1.9 fusion.29
  825.6 2.6 fusion.13
  828.2 1.1 fusion.16
  830.4 1.1 fusion.15
  831.5 1.5 pad_maximum_fusion.1
  833.0 2.0 pad_maximum_fusion
  (55 shorter events, 8.1 us)
Async XLA Ops:
  7.2 159.4 %copy-start.8 = (s32[3,64]{1,0:T(4,128)S(1)}, s32[3,64]{1,0:T(4,128)}, u32[]{:S(2)}) copy-start(s32[3,64]{1,0:T(4,128)} %param.7) | copy-start | bytes 2308
  7.2 55.1 %all-gather.9.cloned.1.call-start = ((), (), s32[]{:S(2)}) async-start(), calls=%async_computation.7 | async-start | bytes 2162688 | tf_op jit(solution)/shard_map/all_gather | solution.py:84
  8.8 104.6 %all-gather.7.cloned.1.call-start = ((), (), s32[]{:S(2)}) async-start(), calls=%async_computation.6 | async-start | bytes 2162688 | tf_op jit(solution)/shard_map/all_gather | solution.py:84
  9.6 154.9 %all-gather.11.cloned.1.call-start = ((), (), s32[]{:S(2)}) async-start(), calls=%async_computation.8 | async-start | bytes 2162688 | tf_op jit(solution)/shard_map/all_gather | solution.py:84
  10.3 235.1 %all-reduce.7.cloned.1.call-start = ((), (), s32[]{:S(2)}) async-start(), calls=%async_computation.10 | async-start | bytes 3145728 | tf_op jit(solution)/shard_map/psum | solution.py:13
  166.5 178.5 %reduce-scatter.6.cloned.1.call-start = ((), (), s32[]{:S(2)}) async-start(), calls=%async_computation.4 | async-start | bytes 6488064 | tf_op jit(solution)/shard_map/reduce_scatter | solution.py:109
  252.0 190.1 %reduce-scatter.4.cloned.1.call-start = ((), (), s32[]{:S(2)}) async-start(), calls=%async_computation.3 | async-start | bytes 6488064 | tf_op jit(solution)/shard_map/reduce_scatter | solution.py:109
  258.7 280.7 %reduce-scatter.8.cloned.1.call-start = ((), (), s32[]{:S(2)}) async-start(), calls=%async_computation.5 | async-start | bytes 6488064 | tf_op jit(solution)/shard_map/reduce_scatter | solution.py:109
  264.4 177.7 %copy-start = (bf16[2,512,512]{2,1,0:T(8,128)(2,1)S(1)}, bf16[2,512,512]{2,1,0:T(8,128)(2,1)}, u32[]{:S(2)}) copy-start(bf16[2,512,512]{2,1,0:T(8,128)(2,1)} %param.8) | copy-start | bytes 3145732
  264.4 558.7 %all-reduce.5.cloned.1.call-start = ((), (), s32[]{:S(2)}) async-start(), calls=%async_computation.9 | async-start | bytes 10485760 | tf_op jit(solution)/shard_map/psum | solution.py:76
  443.5 100.7 %copy-start.2 = (f32[96,512]{1,0:T(8,128)S(1)}, f32[96,512]{1,0:T(8,128)}, u32[]{:S(2)}) copy-start(f32[96,512]{1,0:T(8,128)} %reduce-scatter.4.cloned.1.call-done) | copy-start | bytes 589828
  540.7 5.1 copy-start.4
  540.7 5.1 copy-start.5
  823.0 2.5 copy-start.1
  825.0 3.2 copy-start.7
  828.2 1.2 copy-start.3
  828.2 2.2 copy-start.6
Sparse Core Ops, SparseCore 0:
  11.1 51.0 all-gather.8
  65.4 47.9 all-gather.6
  116.5 47.9 all-gather.10
  167.0 78.4 all-reduce.6
  252.1 92.8 reduce-scatter.5
  348.9 93.1 reduce-scatter.3
  446.1 93.2 reduce-scatter.7
  547.8 275.1 all-reduce.4
where the time goes:
time: 843 us; the launch traced here: 842 us
  waiting for transfers between devices  747 us (89%)
  matrix products  35.6 us (4%)
  between operations  29.7 us (4%)
  other arithmetic  16.8 us (2%)
  local copies, waits for them, and re-layouts  12.5 us (1%)
    psum x1, waiting for transfers between devices, node_sums(): return lax.psum((first_part, second_part), ('row', 'col'))  275 us
    reduce_scatter x3, waiting for transfers between devices, on_device(): lax.psum_scatter(jnp.dot(columns, weights, preferred_element_type=jnp.flo...  255 us
    all_gather x3, waiting for transfers between devices, on_device(): row_slots = lax.all_gather(factor_slots[node], 'col', axis=0, tiled=True)  150 us
    psum x1, waiting for transfers between devices, spread(): return lax.psum(jnp.where(mine, shard, jnp.zeros_like(shard)), axis)  66 us
    dot_general x3, matrix products, on_device(): jnp.dot(columns, weights, preferred_element_type=jnp.float32)  18.5 us
  transfers between devices with their start and end apart: 8, of which 8 were waited for; matrix products, arithmetic and copies ran while one was open for 4% of the time, Pallas kernels for 0%

commit v1 on v0

--- a/solution.py
+++ b/solution.py
@@ -71,9 +71,13 @@
         return (diagonal, upper)
 
     def node_sums(node, first_part, second_part):
+
+        def list_surface(original):
+            return jax.lax.psum(jax.lax.psum(original, "row"), "col")
+
         if node == 0:
             return (lax.psum(first_part, ("row", "col")), None)
-        return lax.psum((first_part, second_part), ("row", "col"))
+        return list_surface((first_part, second_part))
 
     panels = []
     diagonals = []

time: 843 us -> 1060 us (1.26)
  waiting for transfers between devices: 747 us -> 964 us
    psum x1 -> x3, waiting for transfers between devices: 275 us -> 485 us  [the longest x1 262 us: node_sums(): return (lax.psum(first_part, ('row', 'col')), None)]
  transfers between devices with their start and end apart: 8 -> 10, of which waited for: 8 -> 10; matrix products, arithmetic and copies ran while one was open for 4% -> 4% of each run, Pallas kernels for 0% -> 0%
where the time goes in v1:
time: 1060 us
  waiting for transfers between devices  964 us (91%)
  matrix products  35.8 us (3%)
  between operations  29.5 us (3%)
  other arithmetic  15.8 us (1%)
  local copies, waits for them, and re-layouts  11.8 us (1%)
    psum x1, waiting for transfers between devices, node_sums(): return (lax.psum(first_part, ('row', 'col')), None)  262 us
    reduce_scatter x3, waiting for transfers between devices, on_device(): lax.psum_scatter(jnp.dot(columns, weights, preferred_element_type=jnp.flo...  261 us
    psum x2, waiting for transfers between devices, list_surface(): return jax.lax.psum(jax.lax.psum(original, 'row'), 'col')  223 us
    all_gather x3, waiting for transfers between devices, on_device(): row_slots = lax.all_gather(factor_slots[node], 'col', axis=0, tiled=True)  150 us
    psum x1, waiting for transfers between devices, spread(): return lax.psum(jnp.where(mine, shard, jnp.zeros_like(shard)), axis)  66 us
  transfers between devices with their start and end apart: 10, of which 10 were waited for; matrix products, arithmetic and copies ran while one was open for 4% of the time, Pallas kernels for 0%

profile of v1, /device:TPU:8, one launch (start us, length us, event | category | flops | bytes accessed | tf_op | source)
XLA Modules:
  0.0 1057.4 jit_solution(1068102721218105848)
XLA Ops:
  7.2 1.6 fusion.71
  10.4 51.9 %all-gather.9.cloned.1.call-done = bf16[1,2048,512]{2,1,0:T(8,128)(2,1)} async-done(((bf16[1,64,512]{2,1,0:T(8,128)(2,1)}), bf16[1,2048,512]{2,1,0:T(8,128)(2,1)}) %all-gather.9.cloned.1.call-update) | async-done | bytes 2097168 | tf_op jit(solution)/shard_map/all_gather | solution.py:88
  62.3 1.9 select_bitcast_fusion.1
  64.2 49.2 %all-gather.7.cloned.1.call-done = bf16[1,2048,512]{2,1,0:T(8,128)(2,1)} async-done(((bf16[1,64,512]{2,1,0:T(8,128)(2,1)}), bf16[1,2048,512]{2,1,0:T(8,128)(2,1)}) %all-gather.7.cloned.1.call-update) | async-done | bytes 2097168 | tf_op jit(solution)/shard_map/all_gather | solution.py:88
  113.4 1.9 select_bitcast_fusion.2
  115.3 49.2 %all-gather.11.cloned.1.call-done = bf16[1,2048,512]{2,1,0:T(8,128)(2,1)} async-done(((bf16[1,64,512]{2,1,0:T(8,128)(2,1)}), bf16[1,2048,512]{2,1,0:T(8,128)(2,1)}) %all-gather.11.cloned.1.call-update) | async-done | bytes 2097168 | tf_op jit(solution)/shard_map/all_gather | solution.py:88
  164.5 1.9 select_bitcast_fusion
  172.6 6.8 constant_dynamic-slice_fusion.4
  179.4 66.0 %all-reduce.14.cloned.1.call-done = (bf16[512,512]{1,0:T(8,128)(2,1)}, bf16[512,512]{1,0:T(8,128)(2,1)}, bf16[512,512]{1,0:T(8,128)(2,1)}) async-done(((bf16[512,512]{1,0:T(8,128)(2,1)}, bf16[512,512]{1,0:T(8,128)(2,1)}, bf16[512,512]{1,0:T(8,128)(2,1)}), (bf16[512,512]{1,0:T(8,128)(2,1)}, bf16[512,512]{1,0:T(8,128)(2,1)}, bf16[512,512]{1,0:T(8,128)(2,1)})) %all-reduce.14.cloned.1.call-update) | async-done | bytes 1572880 | tf_op jit(solution)/shard_map/psum | solution.py:13
  245.4 6.5 fusion.4
  252.2 6.5 fusion
  258.8 5.5 fusion.8
  272.5 1.2 select_bitcast_fusion.8
  273.7 1.2 select_bitcast_fusion.5
  274.9 70.0 %reduce-scatter.6.cloned.1.call-done = f32[96,512]{1,0:T(8,128)} async-done(((f32[3072,512]{1,0:T(8,128)}), f32[96,512]{1,0:T(8,128)}) %reduce-scatter.6.cloned.1.call-update) | async-done | bytes 196624 | tf_op jit(solution)/shard_map/reduce_scatter | solution.py:113
  345.0 97.1 %reduce-scatter.4.cloned.1.call-done = f32[96,512]{1,0:T(8,128)} async-done(((f32[3072,512]{1,0:T(8,128)}), f32[96,512]{1,0:T(8,128)}) %reduce-scatter.4.cloned.1.call-update) | async-done | bytes 196624 | tf_op jit(solution)/shard_map/reduce_scatter | solution.py:113
  442.1 1.4 convolution_subtract_fusion.1
  443.5 1.7 fusion.69
  445.2 94.2 %reduce-scatter.8.cloned.1.call-done = f32[96,512]{1,0:T(8,128)} async-done(((f32[3072,512]{1,0:T(8,128)}), f32[96,512]{1,0:T(8,128)}) %reduce-scatter.8.cloned.1.call-update) | async-done | bytes 196624 | tf_op jit(solution)/shard_map/reduce_scatter | solution.py:113
  539.4 1.3 convolution_subtract_fusion
  540.7 1.8 fusion.67
  542.5 1.8 fusion.64
  544.2 1.7 fusion.39
  550.4 1.2 select_bitcast_fusion.10
  551.6 1.7 fusion.41
  553.6 101.2 %all-reduce.12.cloned.1.call-done = (f32[512,512]{1,0:T(8,128)}, f32[512,512]{1,0:T(8,128)}, f32[512,512]{1,0:T(8,128)}, f32[512,512]{1,0:T(8,128)}) async-done(((f32[512,512]{1,0:T(8,128)}, f32[512,512]{1,0:T(8,128)}, f32[512,512]{1,0:T(8,128)}, f32[512,512]{1,0:T(8,128)}), (f32[512,512]{1,0:T(8,128)}, f32[512,512]{1,0:T(8,128)}, f32[512,512]{1,0:T(8,128)}, ...) | async-done | bytes 4194320 | tf_op jit(solution)/shard_map/psum | solution.py:76
  655.7 262.0 %all-reduce.8.cloned.1.call-done = f32[512,512]{1,0:T(8,128)} async-done(((f32[512,512]{1,0:T(8,128)}), f32[512,512]{1,0:T(8,128)}) %all-reduce.8.cloned.1.call-update) | async-done | bytes 1048592 | tf_op jit(solution)/shard_map/psum | solution.py:79
  917.7 1.8 fusion.29
  919.5 121.4 %all-reduce.10.cloned.1.call-done = (f32[512,512]{1,0:T(8,128)}, f32[512,512]{1,0:T(8,128)}, f32[512,512]{1,0:T(8,128)}, f32[512,512]{1,0:T(8,128)}) async-done(((f32[512,512]{1,0:T(8,128)}, f32[512,512]{1,0:T(8,128)}, f32[512,512]{1,0:T(8,128)}, f32[512,512]{1,0:T(8,128)}), (f32[512,512]{1,0:T(8,128)}, f32[512,512]{1,0:T(8,128)}, f32[512,512]{1,0:T(8,128)}, ...) | async-done | bytes 4194320 | tf_op jit(solution)/shard_map/psum | solution.py:76
  1040.9 2.7 fusion.13
  1047.1 1.5 pad_maximum_fusion.1
  1048.6 2.0 pad_maximum_fusion
  (59 shorter events, 9.9 us)
Async XLA Ops:
  7.2 159.4 %copy-start.7 = (s32[3,64]{1,0:T(4,128)S(1)}, s32[3,64]{1,0:T(4,128)}, u32[]{:S(2)}) copy-start(s32[3,64]{1,0:T(4,128)} %param.7) | copy-start | bytes 2308
  7.2 55.1 %all-gather.9.cloned.1.call-start = ((), (), s32[]{:S(2)}) async-start(), calls=%async_computation.8 | async-start | bytes 2162688 | tf_op jit(solution)/shard_map/all_gather | solution.py:88
  8.8 104.6 %all-gather.7.cloned.1.call-start = ((), (), s32[]{:S(2)}) async-start(), calls=%async_computation.7 | async-start | bytes 2162688 | tf_op jit(solution)/shard_map/all_gather | solution.py:88
  9.6 154.9 %all-gather.11.cloned.1.call-start = ((), (), s32[]{:S(2)}) async-start(), calls=%async_computation.9 | async-start | bytes 2162688 | tf_op jit(solution)/shard_map/all_gather | solution.py:88
  10.3 235.1 %all-reduce.14.cloned.1.call-start = ((), (), s32[]{:S(2)}) async-start(), calls=%async_computation.12 | async-start | bytes 3145728 | tf_op jit(solution)/shard_map/psum | solution.py:13
  166.5 178.5 %reduce-scatter.6.cloned.1.call-start = ((), (), s32[]{:S(2)}) async-start(), calls=%async_computation.4 | async-start | bytes 6488064 | tf_op jit(solution)/shard_map/reduce_scatter | solution.py:113
  252.0 190.1 %reduce-scatter.4.cloned.1.call-start = ((), (), s32[]{:S(2)}) async-start(), calls=%async_computation.3 | async-start | bytes 6488064 | tf_op jit(solution)/shard_map/reduce_scatter | solution.py:113
  258.7 280.7 %reduce-scatter.8.cloned.1.call-start = ((), (), s32[]{:S(2)}) async-start(), calls=%async_computation.5 | async-start | bytes 6488064 | tf_op jit(solution)/shard_map/reduce_scatter | solution.py:113
  264.3 177.8 %copy-start = (bf16[2,512,512]{2,1,0:T(8,128)(2,1)S(1)}, bf16[2,512,512]{2,1,0:T(8,128)(2,1)}, u32[]{:S(2)}) copy-start(bf16[2,512,512]{2,1,0:T(8,128)(2,1)} %param.8) | copy-start | bytes 3145732
  264.4 390.5 %all-reduce.12.cloned.1.call-start = ((), (), s32[]{:S(2)}) async-start(), calls=%async_computation.11 | async-start | bytes 8388608 | tf_op jit(solution)/shard_map/psum | solution.py:76
  443.5 100.7 %copy-start.3 = (f32[96,512]{1,0:T(8,128)S(1)}, f32[96,512]{1,0:T(8,128)}, u32[]{:S(2)}) copy-start(f32[96,512]{1,0:T(8,128)} %reduce-scatter.4.cloned.1.call-done) | copy-start | bytes 589828
  545.9 371.7 %all-reduce.8.cloned.1.call-start = ((), (), s32[]{:S(2)}) async-start(), calls=%async_computation.6 | async-start | bytes 2097152 | tf_op jit(solution)/shard_map/psum | solution.py:79
  553.3 487.6 %all-reduce.10.cloned.1.call-start = ((), (), s32[]{:S(2)}) async-start(), calls=%async_computation.10 | async-start | bytes 8388608 | tf_op jit(solution)/shard_map/psum | solution.py:76
  917.7 123.3 %copy-start.2 = (f32[512,512]{1,0:T(8,128)S(1)}, f32[512,512]{1,0:T(8,128)}, u32[]{:S(2)}) copy-start(f32[512,512]{1,0:T(8,128)} %all-reduce.8.cloned.1.call-done) | copy-start | bytes 3145732
  1040.9 2.7 copy-start.1
  1040.9 2.8 copy-start.6
  1043.7 1.2 copy-start.4
  1043.7 2.2 copy-start.5
Sparse Core Ops, SparseCore 0:
  11.1 51.0 all-gather.8
  65.4 47.9 all-gather.6
  116.5 47.9 all-gather.10
  167.0 78.4 all-reduce.13
  252.1 92.8 reduce-scatter.5
  348.9 93.1 reduce-scatter.3
  446.1 93.2 reduce-scatter.7
  546.1 108.7 all-reduce.11
  660.3 257.3 all-reduce.7
  921.0 119.8 all-reduce.9
